TPU v7x, 32 devices: a whole 2x2x4 slice. The times are simulated.
32 devices in a mesh: clip: 2 (over x), trow: 8 (over z, y), tcol: 2 (over core).
Axes of the slice: x: 2, y: 2, z: 4, core: 2. Of those that a mesh axis runs over, the one named last changes fastest.
Arguments:
- field: bfloat16 [8, 2048, 8192], P(None, ('clip', 'trow'), 'tcol'), parts along dimension 1, may hold values from -6 to 6
- pointwise: bfloat16 [2, 8, 8], replicated, may hold values from -2 to 2
- mixing: bfloat16 [2, 2, 8, 8, 4608], replicated, may hold values from -2 to 2
- project: bfloat16 [8], replicated, may hold values from -2 to 2
Outputs:
- image: bfloat16 [2048, 8192], P(('clip', 'trow'), 'tcol'), parts along dimension 0
There are 2 independent parts, one for each index of `clip`. A program takes and returns all parts, laid end to end along the dimension named above; an argument that names none is the same for every part. Nothing has to cross between parts.
All inputs are finite; a program needn't handle non-finite values.
Results may differ from a plain program's by a relative error of at most 0.0084.
Values sent between devices are 32-bit elements; how exact they have to be, the bound alone decides.
A program may use at most 128 MiB of HBM per device.

v0:
```python
import functools
import math

import jax
import jax.numpy as jnp
from jax import lax
from jax.experimental import pallas as pl
from jax.experimental.pallas import tpu as pltpu
from jax.sharding import PartitionSpec as P

KY = 48
LAYERS = 2
LANES = 128
SUB = 8
XB = 16
MESH = pl.DeviceIdType.MESH
VMEM_BYTES = 60 * 1024 * 1024


def tile_of(cols):
    for size in (512, 256, 128):
        if cols % size == 0:
            return size
    return cols


def phase_angle(columns, total):
    freqs = jnp.arange(KY, dtype=jnp.int32)
    phase = freqs[:, None] * columns[None, :] % total
    return phase.astype(jnp.float32) * (2.0 * math.pi / total)


def column_seeds(start, count, tile, total):
    coarse = phase_angle(start + jnp.arange(count // LANES, dtype=jnp.int32) * LANES, total)
    coarse = coarse.reshape(KY, count // tile, tile // LANES).transpose(1, 0, 2)
    fine = phase_angle(jnp.arange(LANES, dtype=jnp.int32), total)
    return (
        jnp.concatenate([jnp.cos(coarse), jnp.sin(coarse)], axis=1),
        jnp.concatenate([jnp.cos(fine), jnp.sin(fine)], axis=0),
    )


def row_tables(start, count, total, owners, per, rows):
    owner = jnp.arange(owners * rows, dtype=jnp.int32) // rows
    local = jnp.arange(owners * rows, dtype=jnp.int32) % rows
    index = owner * per + local
    valid = (local < per) & (index < 2 * KY)
    freqs = jnp.where(index < KY, index, index + (total - 2 * KY))
    freqs = jnp.where(valid, freqs, 0)
    places = start + jnp.arange(count, dtype=jnp.int32)
    phase = freqs[:, None] * places[None, :] % total
    angle = phase.astype(jnp.float32) * (2.0 * math.pi / total)
    keep = valid[:, None]
    return jnp.where(keep, jnp.cos(angle), 0.0), jnp.where(keep, jnp.sin(angle), 0.0)


def transform_rows(channels, rows_here, scale, table_ref, acc, out_ref):
    cores, groups = out_ref.shape[:2]
    out_ref[...] = jnp.zeros_like(out_ref)
    for c in range(channels):
        sums = acc[:, c * rows_here : (c + 1) * rows_here]
        turned = jnp.concatenate([sums[KY:], -sums[:KY]], axis=0)
        part = lax.dot_general(
            table_ref[...],
            jnp.concatenate([sums, turned], axis=1),
            (((1,), (1,)), ((), ())),
            precision=lax.Precision.HIGHEST,
            preferred_element_type=jnp.float32,
        )
        part = part * scale
        out_ref[:, :, c, :, : 2 * KY] = part.reshape(cores, groups, part.shape[0] // (cores * groups), 2 * KY)


def accumulate(value, table, acc):
    acc[...] += lax.dot_general(
        table, value, (((1,), (1,)), ((), ())), preferred_element_type=jnp.float32
    )


def forward_kernel(scale, field_ref, coarse_ref, fine_ref, table_ref, et_ref, out_ref, acc):
    channels, rows_here, cols = field_ref.shape
    step = pl.program_id(0)

    @pl.when(step == 0)
    def _():
        acc[...] = jnp.zeros_like(acc)

    cos_fine, sin_fine = fine_ref[:KY], fine_ref[KY:]
    for group in range(cols // LANES):
        cos_coarse = coarse_ref[0, :KY, group : group + 1]
        sin_coarse = coarse_ref[0, KY:, group : group + 1]
        cosine = cos_coarse * cos_fine - sin_coarse * sin_fine
        sine = sin_coarse * cos_fine + cos_coarse * sin_fine
        et_ref[:, group * LANES : (group + 1) * LANES] = jnp.concatenate([cosine, -sine], axis=0).astype(jnp.bfloat16)
    accumulate(field_ref[...].reshape(channels * rows_here, cols), et_ref[...], acc)

    @pl.when(step == pl.num_programs(0) - 1)
    def _():
        transform_rows(channels, rows_here, scale, table_ref, acc, out_ref)


def prepare_hidden(y_ref, inverse_ref, hidden):
    channels = y_ref.shape[2]
    rows_here = inverse_ref.shape[0]
    depth = inverse_ref.shape[1] // 2
    lane = lax.broadcasted_iota(jnp.int32, (depth, LANES), 1)
    for o in range(channels):
        here = y_ref[:, :, o].reshape(depth, LANES)
        turned = jnp.where(lane < KY, -pltpu.roll(here, LANES - KY, 1), pltpu.roll(here, KY, 1))
        turned = jnp.where(lane < 2 * KY, turned, 0.0)
        part = jnp.dot(
            inverse_ref[...],
            jnp.concatenate([here, turned], axis=0),
            precision=lax.Precision.HIGHEST,
            preferred_element_type=jnp.float32,
        ).astype(jnp.bfloat16)
        for block in range(rows_here // XB):
            start = (block * channels + o) * XB
            hidden[start : start + XB, :] = part[block * XB : (block + 1) * XB, : 2 * KY]


def pointwise_matrix(layer, channels, weights_ref, kron):
    row = lax.broadcasted_iota(jnp.int32, (XB, channels * XB), 0)
    lane = lax.broadcasted_iota(jnp.int32, (XB, channels * XB), 1)
    for o in range(channels):
        value = jnp.zeros((XB, channels * XB), jnp.float32)
        for c in range(channels):
            value = jnp.where(lane == row + c * XB, weights_ref[layer * channels + o, c], value)
        kron[o * XB : (o + 1) * XB, :] = value.astype(jnp.bfloat16)


def spectral_values(et_ref, hidden, spectral):
    spectral[...] = jnp.dot(hidden[...], et_ref[...], preferred_element_type=jnp.float32)


def block_update(block, value_ref, kron, spectral):
    channels, _, cols = value_ref.shape
    size = channels * XB
    value = value_ref[:, block * XB : (block + 1) * XB, :].reshape(size, cols)
    local = jnp.dot(kron[...], value, preferred_element_type=jnp.float32)
    return jnp.tanh(local + spectral[block * size : (block + 1) * size, :] * (1.0 / KY))


def middle_kernel(
    layer, scale, value_ref, et_ref, y_ref, inverse_ref, weights_ref, table_ref, next_ref, out_ref, kron, hidden, spectral, acc
):
    channels, rows_here, cols = value_ref.shape
    step = pl.program_id(0)

    @pl.when(step == 0)
    def _():
        acc[...] = jnp.zeros_like(acc)
        prepare_hidden(y_ref, inverse_ref, hidden)
        pointwise_matrix(layer, channels, weights_ref, kron)

    spectral_values(et_ref, hidden, spectral)
    for block in range(rows_here // XB):
        updated = block_update(block, value_ref, kron, spectral).astype(jnp.bfloat16)
        next_ref[:, block * XB : (block + 1) * XB, :] = updated.reshape(channels, XB, cols)
    accumulate(next_ref[...].reshape(channels * rows_here, cols), et_ref[...], acc)

    @pl.when(step == pl.num_programs(0) - 1)
    def _():
        transform_rows(channels, rows_here, scale, table_ref, acc, out_ref)


def last_kernel(layer, value_ref, et_ref, y_ref, inverse_ref, weights_ref, image_ref, kron, hidden, spectral):
    channels, rows_here, cols = value_ref.shape

    @pl.when(pl.program_id(0) == 0)
    def _():
        prepare_hidden(y_ref, inverse_ref, hidden)
        pointwise_matrix(layer, channels, weights_ref, kron)

    spectral_values(et_ref, hidden, spectral)
    for block in range(rows_here // XB):
        updated = block_update(block, value_ref, kron, spectral).reshape(channels, XB, cols)
        total = weights_ref[LAYERS * channels, 0] * updated[0]
        for c in range(1, channels):
            total = total + weights_ref[LAYERS * channels, c] * updated[c]
        image_ref[block * XB : (block + 1) * XB, :] = total.astype(jnp.bfloat16)


def exchange_kernel(
    groups, per, layer, spectrum_ref, same_ref, cross_ref, out_ref, partner_part, mine, arrived, mixed,
    pair_send, pair_recv, sum_send, sum_recv, mix_send, mix_recv, relay_send, relay_recv,
):
    clip = lax.axis_index("clip")
    row = lax.axis_index("trow")
    core = lax.axis_index("tcol")
    other = 1 - core
    channels = spectrum_ref.shape[2]

    if per < spectrum_ref.shape[3]:
        partner_part[...] = jnp.zeros_like(partner_part)
        arrived[...] = jnp.zeros_like(arrived)
        out_ref[...] = jnp.zeros_like(out_ref)

    barrier = pltpu.get_barrier_semaphore()
    pl.semaphore_signal(barrier, inc=1, device_id=(clip, row, other), device_id_type=MESH)
    for j in range(1, groups):
        peer = lax.rem(row + j, groups)
        pl.semaphore_signal(barrier, inc=1, device_id=(clip, peer, core), device_id_type=MESH)
    pl.semaphore_wait(barrier, groups)

    def used(ref):
        return ref.at[:, pl.ds(0, per), :]

    pairs = []
    for j in range(1, groups + 1):
        peer = lax.rem(row + j, groups)
        copy = pltpu.make_async_remote_copy(
            src_ref=used(spectrum_ref.at[other, peer]),
            dst_ref=used(partner_part.at[peer]),
            send_sem=pair_send.at[j - 1],
            recv_sem=pair_recv.at[j - 1],
            device_id=(clip, row, other),
            device_id_type=MESH,
        )
        copy.start()
        pairs.append(copy)
    sums = []
    for j in range(1, groups + 1):
        peer = lax.rem(row + j, groups)
        pairs[j - 1].wait_recv()
        mine[peer] = spectrum_ref[core, peer] + partner_part[peer]
        if j < groups:
            copy = pltpu.make_async_remote_copy(
                src_ref=used(mine.at[peer]),
                dst_ref=used(arrived.at[j - 1]),
                send_sem=sum_send.at[j - 1],
                recv_sem=sum_recv.at[j - 1],
                device_id=(clip, peer, core),
                device_id_type=MESH,
            )
            copy.start()
            sums.append(copy)
    total = mine[row]
    for j in range(1, groups):
        sums[j - 1].wait_recv()
        total = total + arrived[j - 1]

    lane = lax.broadcasted_iota(jnp.int32, total.shape[1:], 1)
    plain = [total[c] for c in range(channels)]
    swapped = [
        jnp.where(lane < KY, pltpu.roll(s, LANES - KY, 1), pltpu.roll(s, KY, 1)) for s in plain
    ]
    for o in range(channels):
        value = same_ref[layer, o, 0] * plain[0] + cross_ref[layer, o, 0] * swapped[0]
        for c in range(1, channels):
            value = value + (same_ref[layer, o, c] * plain[c] + cross_ref[layer, o, c] * swapped[c])
        mixed[o] = value
    out_ref[core, row] = mixed[...]

    sends = []
    for j in range(1, groups):
        peer = lax.rem(row + j, groups)
        copy = pltpu.make_async_remote_copy(
            src_ref=used(mixed),
            dst_ref=used(out_ref.at[core, row]),
            send_sem=mix_send.at[j - 1],
            recv_sem=mix_recv.at[j - 1],
            device_id=(clip, peer, core),
            device_id_type=MESH,
        )
        copy.start()
        sends.append(copy)
    relays = []
    for j in range(groups):
        source = lax.rem(row + groups - j, groups)
        if j:
            sends[j - 1].wait_recv()
        relay = pltpu.make_async_remote_copy(
            src_ref=used(mixed if j == 0 else out_ref.at[core, source]),
            dst_ref=used(out_ref.at[core, source]),
            send_sem=relay_send.at[j],
            recv_sem=relay_recv.at[j],
            device_id=(clip, row, other),
            device_id_type=MESH,
        )
        relay.start()
        relays.append(relay)
    for copy in pairs + sums + sends:
        copy.wait_send()
    for relay in relays:
        relay.wait()


def whole(shape):
    return pl.BlockSpec(shape, lambda i: (0,) * len(shape))


def exchange(spectrum, same, cross, groups, per, cid):
    chunk = spectrum.shape[2:]
    dma = pltpu.SemaphoreType.DMA
    vmem = pl.BlockSpec(memory_space=pltpu.VMEM)
    links = max(groups - 1, 1)
    return pl.pallas_call(
        functools.partial(exchange_kernel, groups, per, cid),
        out_shape=jax.ShapeDtypeStruct(spectrum.shape, jnp.float32),
        in_specs=[vmem, vmem, vmem],
        out_specs=vmem,
        scratch_shapes=[
            pltpu.VMEM((groups,) + chunk, jnp.float32),
            pltpu.VMEM((groups,) + chunk, jnp.float32),
            pltpu.VMEM((links,) + chunk, jnp.float32),
            pltpu.VMEM(chunk, jnp.float32),
            dma((groups,)), dma((groups,)), dma((links,)), dma((links,)), dma((links,)), dma((links,)),
            dma((groups,)), dma((groups,)),
        ],
        compiler_params=pltpu.CompilerParams(
            collective_id=cid, has_side_effects=True, vmem_limit_bytes=VMEM_BYTES
        ),
        name=f"exchange_{cid}",
    )(spectrum, same, cross)


def body(groups, cores, field, pointwise, mixing, project):
    channels, rows_here, cols_here = field.shape
    total_rows = rows_here * groups
    total_cols = cols_here * cores
    row_index = lax.axis_index("trow")
    core_index = lax.axis_index("tcol")
    owners = groups * cores
    per = min(p for p in range(1, 2 * KY + 1) if 2 * KY % p == 0 and p * owners >= 2 * KY)
    sub = -(-per // SUB) * SUB
    scale = 1.0 / math.sqrt(total_rows * total_cols)
    tile = tile_of(cols_here)
    steps = cols_here // tile

    coarse, fine = column_seeds(core_index * cols_here, cols_here, tile, total_cols)
    cosine, sine = row_tables(row_index * rows_here, rows_here, total_rows, owners, per, sub)
    forward_table = jnp.concatenate([cosine, sine], axis=1)
    inverse_table = jnp.concatenate([cosine.T, sine.T], axis=1)

    first = (core_index * groups + row_index) * (per * KY)
    chunk = lax.dynamic_slice_in_dim(mixing, first, per * KY, 4)
    chunk = chunk.reshape(LAYERS, 2, channels, channels, per, KY).astype(jnp.float32)
    widths = ((0, 0), (0, 0), (0, 0), (0, sub - per), (0, LANES - 2 * KY))
    same = jnp.pad(jnp.concatenate([chunk[:, 0], chunk[:, 0]], axis=-1), widths)
    cross = jnp.pad(jnp.concatenate([-chunk[:, 1], chunk[:, 1]], axis=-1), widths)
    weights = jnp.concatenate([pointwise.reshape(LAYERS * channels, channels), project[None]], axis=0)
    weights = weights.astype(jnp.float32)

    spectrum_shape = (cores, groups, channels, sub, LANES)
    spectrum_type = jax.ShapeDtypeStruct(spectrum_shape, jnp.float32)
    value_spec = pl.BlockSpec((channels, rows_here, tile), lambda i: (0, 0, i))
    et_spec = pl.BlockSpec((2 * KY, tile), lambda i: (0, i))
    smem = pl.BlockSpec(memory_space=pltpu.SMEM)
    kron = pltpu.VMEM((channels * XB, channels * XB), jnp.bfloat16)
    hidden = pltpu.VMEM((channels * rows_here, 2 * KY), jnp.bfloat16)
    spectral = pltpu.VMEM((channels * rows_here, tile), jnp.float32)
    acc = pltpu.VMEM((2 * KY, channels * rows_here), jnp.float32)
    params = pltpu.CompilerParams(dimension_semantics=("arbitrary",), vmem_limit_bytes=VMEM_BYTES)

    columns, spectrum = pl.pallas_call(
        functools.partial(forward_kernel, scale),
        grid=(steps,),
        out_shape=(jax.ShapeDtypeStruct((2 * KY, cols_here), jnp.bfloat16), spectrum_type),
        in_specs=[
            value_spec,
            pl.BlockSpec((1,) + coarse.shape[1:], lambda i: (i, 0, 0)),
            whole(fine.shape),
            whole(forward_table.shape),
        ],
        out_specs=(et_spec, whole(spectrum_shape)),
        scratch_shapes=[acc],
        compiler_params=params,
        name="forward",
    )(field, coarse, fine, forward_table)

    current = field
    for layer in range(LAYERS):
        y = exchange(spectrum, same, cross, groups, per, layer)
        specs = [value_spec, et_spec, whole(spectrum_shape), whole(inverse_table.shape), smem]
        if layer + 1 < LAYERS:
            current, spectrum = pl.pallas_call(
                functools.partial(middle_kernel, layer, scale),
                grid=(steps,),
                out_shape=(jax.ShapeDtypeStruct(field.shape, jnp.bfloat16), spectrum_type),
                in_specs=specs + [whole(forward_table.shape)],
                out_specs=(value_spec, whole(spectrum_shape)),
                scratch_shapes=[kron, hidden, spectral, acc],
                compiler_params=params,
                name="middle",
            )(current, columns, y, inverse_table, weights, forward_table)
        else:
            image = pl.pallas_call(
                functools.partial(last_kernel, layer),
                grid=(steps,),
                out_shape=jax.ShapeDtypeStruct((rows_here, cols_here), jnp.bfloat16),
                in_specs=specs,
                out_specs=pl.BlockSpec((rows_here, tile), lambda i: (0, i)),
                scratch_shapes=[kron, hidden, spectral],
                compiler_params=params,
                name="last",
            )(current, columns, y, inverse_table, weights)
    return image


def solution(mesh):
    groups, cores = mesh.shape["trow"], mesh.shape["tcol"]
    in_specs = (P(None, ("clip", "trow"), "tcol"), P(), P(), P())
    out_specs = P(("clip", "trow"), "tcol")
    return jax.shard_map(
        functools.partial(body, groups, cores), mesh=mesh, in_specs=in_specs, out_specs=out_specs, check_vma=False
    )
```

profile of v0, /device:TPU:0, one launch (start us, length us, event | category | flops | bytes accessed | tf_op | source)
XLA Modules:
  0.0 85.8 jit_solution(15134524676701843671)
XLA Ops:
  0.0 1.3 %maximum_convert_fusion.weights_ref = f32[17,8]{1,0:T(8,128)} fusion(bf16[1,8]{1,0:T(2,128)(2,1)} %bitcast.15, bf16[16,8]{1,0:T(8,128)(2,1)} %bitcast.14), kind=kLoop, calls=%fused_computation.53 | loop fusion | flops 544 | bytes 816 | tf_op jit(solution)/shard_map/convert_element_type | solution.py:343
  1.3 0.1 fusion.21
  1.5 0.1 pad_maximum_fusion.3
  1.6 0.1 fusion.18
  1.7 0.6 pad_maximum_fusion.2.fine_ref
  2.3 0.6 cosine_select_fusion
  2.9 0.7 pad_maximum_fusion
  3.7 0.9 %copy.18.coarse_ref = f32[8,96,4]{2,1,0:T(8,128)} copy(f32[8,96,4]{1,0,2:T(8,128)S(1)} %pad_maximum_fusion.3) | data formatting | bytes 24576 | tf_op jit(solution)/shard_map/concatenate | solution.py:38
  4.6 1.1 %dynamic-slice_convert_fusion = f32[2,2,8,8,288]{4,3,2,1,0:T(8,128)S(1)} fusion(bf16[2,2,8,8,4608]{4,3,2,1,0:T(8,128)(2,1)} %param.6, s32[]{:T(128)S(6)} %select_n.116), kind=kLoop, calls=%fused_computation.6 | loop fusion | flops 73728 | bytes 442372 | tf_op jit(solution)/shard_map/convert_element_type | solution.py:338
  5.7 0.3 reshape.60
  6.0 0.1 fusion.25
  6.1 0.1 slice_bitcast_fusion
  6.2 1.4 %select_maximum_fusion = (f32[2,8,8,8,128]{4,3,2,1,0:T(8,128)}, f32[2,8,8,8,128]{4,3,2,1,0:T(8,128)}) fusion(f32[2,8,8,6,48]{4,3,2,1,0:T(8,128)S(1)} %get-tuple-element.13, f32[2,8,8,6,48]{4,3,2,1,0:T(8,128)S(1)} %fusion.25, f32[2,8,8,6,48]{4,3,2,1,0:T(8,128)S(1)} %get-tuple-element.14), kind=kLoop, calls=%fused_computation | loop fusion | flops 1703936 | bytes 1490944 | tf_op jit(solution)/shard_map/concatenate | solution.py:341
  7.5 9.8 %forward.1 = (bf16[96,4096]{1,0:T(8,128)(2,1)}, f32[2,8,8,8,128]{4,3,2,1,0:T(8,128)}) custom-call(bf16[8,128,4096]{2,1,0:T(8,128)(2,1)} %value_ref.1, f32[8,96,4]{2,1,0:T(8,128)} %copy.18.coarse_ref, f32[96,128]{1,0:T(8,128)} %pad_maximum_fusion.2.fine_ref, f32[128,256]{1,0:T(8,128)} %get-tuple-element.23.table_ref), custom_call_target="tpu_custom_call" | custom-call | tf_op jit(solution)/shard_map/forward/pallas_call | solution.py:356
  17.3 21.6 %exchange_0.1.y_ref = f32[2,8,8,8,128]{4,3,2,1,0:T(8,128)} custom-call(f32[2,8,8,8,128]{4,3,2,1,0:T(8,128)} %get-tuple-element.10.spectrum_ref, f32[2,8,8,8,128]{4,3,2,1,0:T(8,128)} %get-tuple-element.26.same_ref, f32[2,8,8,8,128]{4,3,2,1,0:T(8,128)} %get-tuple-element.25.cross_ref), custom_call_target="tpu_custom_call" | custom-call | tf_op jit(solution)/shard_map/exchange_0/pallas_call | solution.py:298
  39.0 15.5 %middle.1 = (bf16[8,128,4096]{2,1,0:T(8,128)(2,1)}, f32[2,8,8,8,128]{4,3,2,1,0:T(8,128)}) custom-call(bf16[8,128,4096]{2,1,0:T(8,128)(2,1)} %value_ref.1, bf16[96,4096]{1,0:T(8,128)(2,1)} %get-tuple-element.9.et_ref, f32[2,8,8,8,128]{4,3,2,1,0:T(8,128)} %exchange_0.1.y_ref, f32[128,256]{1,0:T(8,128)} %get-tuple-element.24.inverse_ref, ...), custom_call_target="tpu_custom_call" | custom-call | tf_op jit(solution)/shard_map/middle/pallas_call | solution.py:377
  54.5 20.0 %exchange_1.1.y_ref = f32[2,8,8,8,128]{4,3,2,1,0:T(8,128)} custom-call(f32[2,8,8,8,128]{4,3,2,1,0:T(8,128)} %get-tuple-element.12.spectrum_ref, f32[2,8,8,8,128]{4,3,2,1,0:T(8,128)} %get-tuple-element.26.same_ref, f32[2,8,8,8,128]{4,3,2,1,0:T(8,128)} %get-tuple-element.25.cross_ref), custom_call_target="tpu_custom_call" | custom-call | tf_op jit(solution)/shard_map/exchange_1/pallas_call | solution.py:298
  74.5 11.3 %last.1 = bf16[128,4096]{1,0:T(8,128)(2,1)} custom-call(bf16[8,128,4096]{2,1,0:T(8,128)(2,1)} %get-tuple-element.11.value_ref, bf16[96,4096]{1,0:T(8,128)(2,1)} %get-tuple-element.9.et_ref, f32[2,8,8,8,128]{4,3,2,1,0:T(8,128)} %exchange_1.1.y_ref, f32[128,256]{1,0:T(8,128)} %get-tuple-element.24.inverse_ref, f32[17,8]{1,0:T(8,128)} %maximum_convert_fusion.weights_ref), custom_call_target="tpu_custom_call" | custom-call | tf_op jit(solution)/shard_map/last/pallas_call | solution.py:388
  (4 shorter events, 0.0 us)
where the time goes:
time: 86.6 us; the launch traced here: 85.8 us
  Pallas kernels  78.2 us (90%)
  other arithmetic  6.14 us (7%)
  local copies, waits for them, and re-layouts  1.35 us (2%)
    pallas_call x2, Pallas kernels, exchange(): pl.pallas_call(functools.partial(exchange_kernel, groups, per, cid), out_...  41.6 us
    pallas_call x1, Pallas kernels, body(): pl.pallas_call(functools.partial(middle_kernel, layer, scale), grid=(step...  15.5 us
    pallas_call x1, Pallas kernels, body(): pl.pallas_call(functools.partial(last_kernel, layer), grid=(steps,), out_...  11.3 us
    pallas_call x1, Pallas kernels, body(): pl.pallas_call(functools.partial(forward_kernel, scale), grid=(steps,), o...  9.77 us

commit v1 on v0

v1 whole, which is shorter than its diff:
```python
import functools
import math

import jax
import jax.numpy as jnp
import numpy as np
from jax import lax
from jax.experimental import pallas as pl
from jax.experimental.pallas import tpu as pltpu
from jax.sharding import PartitionSpec as P

KY = 48
LAYERS = 2
LANES = 128
HALVES = 2
QUAD = 4
TRIO = 3
XB = 32
MESH = pl.DeviceIdType.MESH
VMEM_BYTES = 62 * 1024 * 1024
BF16, F32 = jnp.bfloat16, jnp.float32
NT = (((1,), (1,)), ((), ()))


def column_constant(total, cores):
    columns = np.arange(total, dtype=np.int64)
    phase = np.arange(KY, dtype=np.int64)[:, None] * columns[None, :] % total
    angle = (phase.astype(np.float32) * np.float32(2.0 * math.pi / total)).astype(np.float64)
    table = np.concatenate([np.cos(angle), -np.sin(angle)], axis=0).astype(np.float32)
    return table.reshape(2 * KY, cores, total // cores).transpose(1, 0, 2).astype(jnp.bfloat16)


def row_constants(total, rows, groups, owners, per, sub):
    index = np.arange(owners)[:, None] * per + np.arange(sub)[None, :]
    valid = (np.arange(sub)[None, :] < per).repeat(owners, 0).reshape(-1)
    index = index.reshape(-1)
    freqs = np.where(index < KY, index, index - 2 * KY)
    keep = valid.astype(np.float64)

    def both(places):
        angle = 2.0 * math.pi * ((freqs[None, :] * places[:, None]) % total) / total
        return np.cos(angle) * keep, np.sin(angle) * keep

    fine = np.stack(both(np.arange(rows, dtype=np.int64))).astype(np.float32)
    coarse = np.stack(both(np.arange(groups, dtype=np.int64) * rows), axis=1)
    coarse = np.pad(coarse, ((0, 0), (0, 6), (0, 0))).astype(np.float32)
    return fine, coarse


def split(value):
    high = value.astype(BF16)
    return high, (value - high.astype(F32)).astype(BF16)


def turned(value):
    lane = lax.broadcasted_iota(jnp.int32, value.shape, 1)
    up = pltpu.roll(value, LANES - KY, 1)
    down = pltpu.roll(value, KY, 1)
    return jnp.where(lane < KY, up, jnp.where(lane < 2 * KY, -down, 0.0))


def pack(parts):
    lane = lax.broadcasted_iota(jnp.int32, parts[0].shape, 1)
    return [
        jnp.where(lane < 2 * KY, parts[j], pltpu.roll(parts[TRIO], 2 * KY - 32 * j, 1)) for j in range(TRIO)
    ]


def unpack(rows):
    lane = lax.broadcasted_iota(jnp.int32, rows[0].shape, 1)
    fourth = jnp.where(
        lane < 32,
        pltpu.roll(rows[0], 32, 1),
        jnp.where(lane < 64, pltpu.roll(rows[1], 64, 1), pltpu.roll(rows[2], 96, 1)),
    )
    return [jnp.where(lane < 2 * KY, r, 0.0) for r in [*rows, fourth]]


def two_transforms(table, first, second):
    value = jnp.concatenate([first, second], axis=1)
    other = jnp.concatenate([turned(first), turned(second)], axis=1)
    high, low = split(jnp.concatenate([value, other], axis=0))
    both = jnp.dot(table, jnp.concatenate([high, low, high], axis=0), preferred_element_type=F32)
    return both[:, :LANES], both[:, LANES:]


def tile_of(cols):
    for size in (2048, 1024, 512, 256, 128):
        if cols % size == 0:
            return size
    return cols


def kernel(
    plan,
    field_hbm, point_hbm, mixing_hbm, project_hbm, et_hbm, fine_hbm, coarse_hbm,
    image_hbm,
    value, local, et, fine, coarse, point, project, raw, same, cross, kron, ahead, back, acc, hidden, total_image, image,
    packed, partner, mine, arrived, spread,
    field_sem, load_sem, pair_send, pair_recv, sum_send, sum_recv, mix_send, mix_recv, relay_send, relay_recv,
):
    groups, cores, owners, first_owner, per, sub, window, scale = plan
    channels, rows, cols = value.shape
    half_channels = channels // HALVES
    tile = tile_of(cols)
    local_tile = min(tile, 512)
    clip = lax.axis_index("clip")
    row = lax.axis_index("trow")
    core = lax.axis_index("tcol")
    other = 1 - core
    near = jnp.clip(row - first_owner, 0, owners - 1)
    is_owner = jnp.logical_and(row >= first_owner, row < first_owner + owners)
    block = core * owners + near
    start_mode = block * (per * KY)
    offset = lax.rem(start_mode, LANES)
    window_start = pl.multiple_of(start_mode - offset, LANES)

    loads = [
        pltpu.make_async_copy(fine_hbm, fine, load_sem.at[0]),
        pltpu.make_async_copy(coarse_hbm.at[row], coarse, load_sem.at[1]),
        pltpu.make_async_copy(et_hbm.at[core], et.at[pl.ds(0, 2 * KY)], load_sem.at[2]),
        pltpu.make_async_copy(point_hbm, point, load_sem.at[3]),
        pltpu.make_async_copy(project_hbm, project, load_sem.at[4]),
        pltpu.make_async_copy(mixing_hbm.at[:, :, :, :, pl.ds(window_start, window)], raw, load_sem.at[5]),
    ]
    for copy in loads[:3]:
        copy.start()

    def field_copy(c):
        return pltpu.make_async_copy(field_hbm.at[c], value.at[c], field_sem.at[c])

    for c in range(channels):
        field_copy(c).start()
    for copy in loads[3:]:
        copy.start()

    arrived[...] = jnp.zeros_like(arrived)
    spread[...] = jnp.zeros_like(spread)
    et[2 * KY :, :] = jnp.zeros((LANES - 2 * KY, cols), BF16)

    barrier = pltpu.get_barrier_semaphore()
    pl.semaphore_signal(barrier, inc=1, device_id=(clip, row, other), device_id_type=MESH)
    for j in range(1, groups):
        peer = lax.rem(row + j, groups)
        pl.semaphore_signal(barrier, inc=1, device_id=(clip, peer, core), device_id_type=MESH)

    def used(ref):
        return ref.at[:, pl.ds(0, per), :]

    loads[0].wait()
    loads[1].wait()
    cc, cs = coarse[0:1, :], coarse[1:2, :]
    cosine = cc * fine[0] - cs * fine[1]
    sine = cs * fine[0] + cc * fine[1]
    high, low = split(jnp.concatenate([cosine, -sine], axis=1))
    back[...] = jnp.concatenate([high, high, low], axis=1)
    high, low = split(jnp.concatenate([cosine.T, sine.T], axis=1) * scale)
    ahead[...] = jnp.concatenate([high, high, low], axis=1)
    loads[2].wait()

    def columns_of(c):
        acc[c] = lax.dot_general(value[c], et[...], NT, preferred_element_type=F32)

    def pair_copy(layer, half):
        return pltpu.make_async_remote_copy(
            src_ref=packed.at[layer, half, other],
            dst_ref=partner.at[layer, half],
            send_sem=pair_send.at[layer, half],
            recv_sem=pair_recv.at[layer, half],
            device_id=(clip, row, other),
            device_id_type=MESH,
        )

    def transform_rows(layer, half):
        parts = []
        for p in range(0, half_channels, 2):
            c = half * half_channels + p
            parts.extend(two_transforms(ahead[...], acc[c], acc[c + 1]))
        for j, rows_j in enumerate(pack(parts)):
            packed[layer, half, :, :, j] = rows_j.reshape(cores, owners, sub, LANES)
        pair_copy(layer, half).start()

    def sum_target(j):
        return lax.rem(near + owners // 2 + j, owners)

    def sum_copy(layer, half, j):
        q = sum_target(j)
        slot = lax.rem(row - (first_owner + q) + groups, groups) - 1
        slot = jnp.maximum(slot, 0)
        return pltpu.make_async_remote_copy(
            src_ref=used(mine.at[layer, half, q]),
            dst_ref=used(arrived.at[layer, half, slot]),
            send_sem=sum_send.at[layer, half, j],
            recv_sem=sum_recv.at[layer, half, slot],
            device_id=(clip, first_owner + q, core),
            device_id_type=MESH,
        )

    def scatter_sums(layer, half):
        pair_copy(layer, half).wait_recv()
        mine[layer, half] = packed[layer, half, core] + partner[layer, half]
        for j in range(owners):
            @pl.when(first_owner + sum_target(j) != row)
            def _():
                sum_copy(layer, half, j).start()

    def spread_copy(layer, half, j):
        return pltpu.make_async_remote_copy(
            src_ref=used(spread.at[layer, half, core, near]),
            dst_ref=used(spread.at[layer, half, core, near]),
            send_sem=mix_send.at[layer, half, j - 1],
            recv_sem=mix_recv.at[layer, half, near],
            device_id=(clip, lax.rem(row + j, groups), core),
            device_id_type=MESH,
        )

    def relay_copy(layer, half, q):
        return pltpu.make_async_remote_copy(
            src_ref=used(spread.at[layer, half, core, q]),
            dst_ref=used(spread.at[layer, half, core, q]),
            send_sem=relay_send.at[layer, half, q],
            recv_sem=relay_recv.at[layer, half, q],
            device_id=(clip, row, other),
            device_id_type=MESH,
        )

    def block_arrival(layer, half, q):
        return pltpu.make_async_remote_copy(
            src_ref=used(spread.at[layer, half, core, q]),
            dst_ref=used(spread.at[layer, half, core, q]),
            send_sem=mix_send.at[layer, half, 0],
            recv_sem=mix_recv.at[layer, half, q],
            device_id=(clip, row, other),
            device_id_type=MESH,
        )

    def partner_arrival(layer, half, q):
        return pltpu.make_async_remote_copy(
            src_ref=used(spread.at[layer, half, other, q]),
            dst_ref=used(spread.at[layer, half, other, q]),
            send_sem=relay_send.at[layer, half, q],
            recv_sem=relay_recv.at[layer, half, q],
            device_id=(clip, row, other),
            device_id_type=MESH,
        )

    def sum_arrival(layer, half, slot):
        return pltpu.make_async_remote_copy(
            src_ref=used(arrived.at[layer, half, slot]),
            dst_ref=used(arrived.at[layer, half, slot]),
            send_sem=sum_send.at[layer, half, 0],
            recv_sem=sum_recv.at[layer, half, slot],
            device_id=(clip, row, other),
            device_id_type=MESH,
        )

    order = sorted(range(1, groups), key=lambda j: abs(2 * j - groups))

    def mix(layer):
        @pl.when(is_owner)
        def _():
            plain = []
            for half in range(HALVES):
                sums = mine[layer, half, near]
                for slot in range(groups - 1):
                    sum_arrival(layer, half, slot).wait_recv()
                    sums = sums + arrived[layer, half, slot]
                plain.extend(unpack([sums[j] for j in range(TRIO)]))
            lane = lax.broadcasted_iota(jnp.int32, plain[0].shape, 1)
            swapped = [
                jnp.where(lane < KY, pltpu.roll(s, LANES - KY, 1), pltpu.roll(s, KY, 1)) for s in plain
            ]
            for half in range(HALVES):
                mixed = []
                for o in range(half * half_channels, (half + 1) * half_channels):
                    at = (layer * channels + o) * channels
                    result = same[at] * plain[0] + cross[at] * swapped[0]
                    for c in range(1, channels):
                        result = result + (same[at + c] * plain[c] + cross[at + c] * swapped[c])
                    mixed.append(result)
                for j, rows_j in enumerate(pack(mixed)):
                    spread[layer, half, core, near, j, 0:per, :] = rows_j[:per]
                for j in order:
                    spread_copy(layer, half, j).start()
                relay_copy(layer, half, near).start()

    def relay(layer, half):
        for q in range(owners):
            @pl.when(first_owner + q != row)
            def _():
                block_arrival(layer, half, q).wait_recv()
                relay_copy(layer, half, q).start()

    def prepare_hidden(layer, half):
        for q in range(owners):
            partner_arrival(layer, half, q).wait_recv()
        parts = unpack([spread[layer, half, :, :, j].reshape(cores * owners * sub, LANES) for j in range(TRIO)])
        for p in range(0, half_channels, 2):
            for k, part in enumerate(two_transforms(back[...], parts[p], parts[p + 1])):
                hidden[half * half_channels + p + k] = part.astype(BF16)

    def kron_matrix(layer):
        size = channels * XB
        spot = lax.broadcasted_iota(jnp.int32, (size, channels), 0) // XB
        pick = (spot == lax.broadcasted_iota(jnp.int32, (size, channels), 1)).astype(F32).astype(BF16)
        wide = jnp.dot(pick, point[layer], preferred_element_type=F32).astype(BF16)
        full = lax.dot_general(wide, pick, NT, preferred_element_type=F32)
        at = lax.rem(lax.broadcasted_iota(jnp.int32, (size, size), 0), XB)
        to = lax.rem(lax.broadcasted_iota(jnp.int32, (size, size), 1), XB)
        kron[layer] = jnp.where(at == to, full, 0.0).astype(BF16)

    def mix_channels(layer):
        def step(i, carry):
            at = pl.multiple_of(i * local_tile, local_tile)
            for b in range(rows // XB):
                piece = value[:, b * XB : (b + 1) * XB, pl.ds(at, local_tile)].reshape(channels * XB, local_tile)
                result = jnp.dot(kron[layer], piece, preferred_element_type=F32)
                local[:, b * XB : (b + 1) * XB, pl.ds(at, local_tile)] = result.reshape(channels, XB, local_tile)
            return carry
        lax.fori_loop(0, cols // local_tile, step, 0)

    def updated(half, at):
        mine_here = slice(half * half_channels, (half + 1) * half_channels)
        lhs = hidden[mine_here].reshape(half_channels * rows, LANES)
        spectral = jnp.dot(lhs, et[:, pl.ds(at, tile)], preferred_element_type=F32)
        spectral = spectral.reshape(half_channels, rows, tile)
        return jnp.tanh(local[mine_here, :, pl.ds(at, tile)] + spectral * (1.0 / KY))

    def update(half):
        def step(i, carry):
            at = pl.multiple_of(i * tile, tile)
            value[half * half_channels : (half + 1) * half_channels, :, pl.ds(at, tile)] = updated(half, at).astype(BF16)
            return carry
        lax.fori_loop(0, cols // tile, step, 0)

    def project_half(half):
        gains = project[...].astype(F32)

        def step(i, carry):
            at = pl.multiple_of(i * tile, tile)
            result = updated(half, at)
            total = None if half == 0 else total_image[:, pl.ds(at, tile)]
            for k in range(half_channels):
                c = half * half_channels + k
                term = gains[0:1, c : c + 1] * result[k]
                total = term if total is None else total + term
            if half + 1 < HALVES:
                total_image[:, pl.ds(at, tile)] = total
            else:
                image[:, pl.ds(at, tile)] = total.astype(BF16)
            return carry
        lax.fori_loop(0, cols // tile, step, 0)

    def prepare_weights():
        loads[5].wait()
        count = LAYERS * 2 * channels
        flat = raw[...].astype(F32).reshape(count * channels, window).astype(BF16)
        mode = lax.broadcasted_iota(jnp.int32, (window, 2 * LANES), 0) - offset
        lane = lax.broadcasted_iota(jnp.int32, (window, 2 * LANES), 1)
        which = lane // LANES
        spot = lane - which * LANES
        wanted = which * KY + jnp.where(spot < KY, spot, spot - KY)
        wanted = jnp.where(spot < 2 * KY, wanted, -window * LANES)
        side = lax.broadcasted_iota(jnp.int32, (LAYERS * channels * channels, LANES), 1)
        for k in range(0, per, 2):
            choose = (mode - k * KY == wanted).astype(F32).astype(BF16)
            picked = jnp.dot(flat, choose, preferred_element_type=F32)
            picked = picked.reshape(LAYERS, 2, channels * channels, 2 * LANES)
            for n in range(2):
                lanes = slice(n * LANES, (n + 1) * LANES)
                real = picked[:, 0, :, lanes].reshape(LAYERS * channels * channels, LANES)
                imag = picked[:, 1, :, lanes].reshape(LAYERS * channels * channels, LANES)
                same[:, k + n, :] = real
                cross[:, k + n, :] = jnp.where(side < KY, -imag, imag)

    def load_and_transform(c, carry):
        field_copy(c).wait()
        columns_of(c)
        return carry

    def transform_only(c, carry):
        columns_of(c)
        return carry

    lax.fori_loop(0, half_channels, load_and_transform, 0)
    pl.semaphore_wait(barrier, groups)
    transform_rows(0, 0)
    lax.fori_loop(half_channels, channels, load_and_transform, 0)
    scatter_sums(0, 0)
    transform_rows(0, 1)
    loads[3].wait()
    loads[4].wait()
    for layer in range(LAYERS):
        kron_matrix(layer)
    scatter_sums(0, 1)
    prepare_weights()

    for layer in range(LAYERS):
        last = layer + 1 == LAYERS
        if last:
            mix_channels(layer)
        mix(layer)
        if not last:
            mix_channels(layer)
        relay(layer, 0)
        prepare_hidden(layer, 0)
        if last:
            project_half(0)
            relay(layer, 1)
            prepare_hidden(layer, 1)
            project_half(1)
        else:
            update(0)
            relay(layer, 1)
            lax.fori_loop(0, half_channels, transform_only, 0)
            transform_rows(layer + 1, 0)
            prepare_hidden(layer, 1)
            update(1)
            scatter_sums(layer + 1, 0)
            lax.fori_loop(half_channels, channels, transform_only, 0)
            transform_rows(layer + 1, 1)
            scatter_sums(layer + 1, 1)

    out = pltpu.make_async_copy(image, image_hbm, load_sem.at[6])
    out.start()
    for layer in range(LAYERS):
        for half in range(HALVES):
            pair_copy(layer, half).wait_send()
            for j in range(owners):
                @pl.when(first_owner + sum_target(j) != row)
                def _():
                    sum_copy(layer, half, j).wait_send()
            for q in range(owners):
                relay_copy(layer, half, q).wait_send()

            @pl.when(is_owner)
            def _():
                for j in order:
                    spread_copy(layer, half, j).wait_send()
    out.wait()


def body(groups, cores, field, pointwise, mixing, project):
    channels, rows, cols = field.shape
    owners = min(4, groups)
    first_owner = (groups - owners) // 2
    per = 2 * KY // (owners * cores)
    sub = -(-per // 8) * 8
    total_rows, total_cols = rows * groups, cols * cores
    scale = 1.0 / math.sqrt(total_rows * total_cols)
    modes = per * KY
    window = max(-(-(b * modes % LANES + modes) // LANES) * LANES for b in range(owners * cores))
    plan = (groups, cores, owners, first_owner, per, sub, window, scale)
    et = jnp.asarray(column_constant(total_cols, cores))
    fine, coarse = row_constants(total_rows, rows, groups, owners * cores, per, sub)
    fine, coarse = jnp.asarray(fine), jnp.asarray(coarse)

    hbm = pl.BlockSpec(memory_space=pl.ANY)
    dma = pltpu.SemaphoreType.DMA
    links = max(groups - 1, 1)
    chunk = (TRIO, sub, LANES)
    pairs = LAYERS * channels * channels
    return pl.pallas_call(
        functools.partial(kernel, plan),
        out_shape=jax.ShapeDtypeStruct((rows, cols), BF16),
        in_specs=[hbm] * 7,
        out_specs=hbm,
        scratch_shapes=[
            pltpu.VMEM((channels, rows, cols), BF16),
            pltpu.VMEM((channels, rows, cols), F32),
            pltpu.VMEM((LANES, cols), BF16),
            pltpu.VMEM(fine.shape, F32),
            pltpu.VMEM(coarse.shape[1:], F32),
            pltpu.VMEM(pointwise.shape, BF16),
            pltpu.VMEM((1, channels), BF16),
            pltpu.VMEM(mixing.shape[:-1] + (window,), BF16),
            pltpu.VMEM((pairs, sub, LANES), F32),
            pltpu.VMEM((pairs, sub, LANES), F32),
            pltpu.VMEM((LAYERS, channels * XB, channels * XB), BF16),
            pltpu.VMEM((cores * owners * sub, 6 * rows), BF16),
            pltpu.VMEM((rows, 6 * cores * owners * sub), BF16),
            pltpu.VMEM((channels, rows, LANES), F32),
            pltpu.VMEM((channels, rows, LANES), BF16),
            pltpu.VMEM((rows, cols), F32),
            pltpu.VMEM((rows, cols), BF16),
            pltpu.VMEM((LAYERS, HALVES, cores, owners) + chunk, F32),
            pltpu.VMEM((LAYERS, HALVES, owners) + chunk, F32),
            pltpu.VMEM((LAYERS, HALVES, owners) + chunk, F32),
            pltpu.VMEM((LAYERS, HALVES, links) + chunk, F32),
            pltpu.VMEM((LAYERS, HALVES, cores, owners) + chunk, F32),
            dma((channels,)), dma((7,)),
            dma((LAYERS, HALVES)), dma((LAYERS, HALVES)),
            dma((LAYERS, HALVES, owners)), dma((LAYERS, HALVES, links)),
            dma((LAYERS, HALVES, links)), dma((LAYERS, HALVES, owners)),
            dma((LAYERS, HALVES, owners)), dma((LAYERS, HALVES, owners)),
        ],
        compiler_params=pltpu.CompilerParams(
            collective_id=0, has_side_effects=True, vmem_limit_bytes=VMEM_BYTES
        ),
        name="operator",
    )(field, pointwise, mixing, project.reshape(1, channels), et, fine, coarse)


def solution(mesh):
    groups, cores = mesh.shape["trow"], mesh.shape["tcol"]
    in_specs = (P(None, ("clip", "trow"), "tcol"), P(), P(), P())
    out_specs = P(("clip", "trow"), "tcol")
    return jax.shard_map(
        functools.partial(body, groups, cores), mesh=mesh, in_specs=in_specs, out_specs=out_specs, check_vma=False
    )
```

time: 86.6 us -> 50.7 us (0.59)
  Pallas kernels: 78.2 us -> 48.2 us
  other arithmetic: 6.14 us -> 0 us
  local copies, waits for them, and re-layouts: 1.35 us -> 2.29 us
    pallas_call x5 -> x1, Pallas kernels: 78.2 us -> 48.2 us  [body(): pl.pallas_call(functools.partial(kernel, plan), out_shape=jax.ShapeDtypeS...]
    concatenate x4 -> x0, other arithmetic: 2.8 us -> none  [the longest x1 1.38 us: body(): jnp.concatenate([-chunk[:, 1], chunk[:, 1]], axis=-1)]
    convert_element_type x2 -> x0, other arithmetic: 2.37 us -> none  [the longest x1 1.31 us: body(): weights = weights.astype(jnp.float32)]
    unnamed x0 -> x1, local copies, waits for them, and re-layouts: none -> 2.29 us
    concatenate x1 -> x0, local copies, waits for them, and re-layouts: 0.94 us -> none  [column_seeds(): jnp.concatenate([jnp.cos(coarse), jnp.sin(coarse)], axis=1)]
where the time goes in v1:
time: 50.7 us; the launch traced here: 50.5 us
  Pallas kernels  48.2 us (95%)
  local copies, waits for them, and re-layouts  2.29 us (5%)
    pallas_call x1, Pallas kernels, body(): pl.pallas_call(functools.partial(kernel, plan), out_shape=jax.ShapeDtypeS...  48.2 us
    unnamed x1, local copies, waits for them, and re-layouts  2.29 us

profile of v1, /device:TPU:0, one launch (start us, length us, event | category | flops | bytes accessed | tf_op | source)
XLA Modules:
  0.0 50.5 jit_solution(10606176184161386542)
XLA Ops:
  0.0 48.2 %operator.1 = bf16[128,4096]{1,0:T(8,128)(2,1)} custom-call(bf16[8,128,4096]{2,1,0:T(8,128)(2,1)} %field_hbm.1, bf16[2,8,8]{2,1,0:T(8,128)(2,1)} %point_hbm.1, bf16[2,2,8,8,4608]{4,3,2,1,0:T(8,128)(2,1)} %mixing_hbm.1, bf16[1,8]{1,0:T(2,128)(2,1)} %bitcast.1, bf16[2,96,4096]{2,1,0:T(8,128)(2,1)} %constant.6.clone.et_hbm, ...), custom_call_target="tpu_custom_call" | custom-call | tf_op jit(solution)/shard_map/operator/pallas_call | solution.py:463
  48.2 2.3 %copy.9 = bf16[128,4096]{1,0:T(8,128)(2,1)} copy(bf16[128,4096]{1,0:T(8,128)(2,1)} %operator.1) | data formatting | bytes 2097152

commit v2 on v1

v2 whole, which is shorter than its diff:
```python
import functools
import math

import jax
import jax.numpy as jnp
import numpy as np
from jax import lax
from jax.experimental import pallas as pl
from jax.experimental.pallas import tpu as pltpu
from jax.sharding import PartitionSpec as P

KY = 48
LAYERS = 2
LANES = 128
HALVES = 2
QUAD = 4
TRIO = 3
XB = 32
MESH = pl.DeviceIdType.MESH
VMEM_BYTES = 62 * 1024 * 1024
BF16, F32 = jnp.bfloat16, jnp.float32
NT = (((1,), (1,)), ((), ()))


def column_constant(total, cores):
    columns = np.arange(total, dtype=np.int64)
    phase = np.arange(KY, dtype=np.int64)[:, None] * columns[None, :] % total
    angle = (phase.astype(np.float32) * np.float32(2.0 * math.pi / total)).astype(np.float64)
    table = np.concatenate([np.cos(angle), -np.sin(angle)], axis=0).astype(np.float32)
    return table.reshape(2 * KY, cores, total // cores).transpose(1, 0, 2).astype(jnp.bfloat16)


def row_constants(total, rows, groups, owners, per, sub):
    index = np.arange(owners)[:, None] * per + np.arange(sub)[None, :]
    valid = (np.arange(sub)[None, :] < per).repeat(owners, 0).reshape(-1)
    index = index.reshape(-1)
    freqs = np.where(index < KY, index, index - 2 * KY)
    keep = valid.astype(np.float64)

    def both(places):
        angle = 2.0 * math.pi * ((freqs[None, :] * places[:, None]) % total) / total
        return np.cos(angle) * keep, np.sin(angle) * keep

    fine = np.stack(both(np.arange(rows, dtype=np.int64))).astype(np.float32)
    coarse = np.stack(both(np.arange(groups, dtype=np.int64) * rows), axis=1)
    coarse = np.pad(coarse, ((0, 0), (0, 6), (0, 0))).astype(np.float32)
    return fine, coarse


def split(value):
    high = value.astype(BF16)
    return high, (value - high.astype(F32)).astype(BF16)


def turned(value):
    lane = lax.broadcasted_iota(jnp.int32, value.shape, 1)
    up = pltpu.roll(value, LANES - KY, 1)
    down = pltpu.roll(value, KY, 1)
    return jnp.where(lane < KY, up, jnp.where(lane < 2 * KY, -down, 0.0))


def pack(parts):
    lane = lax.broadcasted_iota(jnp.int32, parts[0].shape, 1)
    return [
        jnp.where(lane < 2 * KY, parts[j], pltpu.roll(parts[TRIO], 2 * KY - 32 * j, 1)) for j in range(TRIO)
    ]


def unpack(rows):
    lane = lax.broadcasted_iota(jnp.int32, rows[0].shape, 1)
    fourth = jnp.where(
        lane < 32,
        pltpu.roll(rows[0], 32, 1),
        jnp.where(lane < 64, pltpu.roll(rows[1], 64, 1), pltpu.roll(rows[2], 96, 1)),
    )
    return [jnp.where(lane < 2 * KY, r, 0.0) for r in [*rows, fourth]]


def two_transforms(table, first, second):
    value = jnp.concatenate([first, second], axis=1)
    other = jnp.concatenate([turned(first), turned(second)], axis=1)
    high, low = split(jnp.concatenate([value, other], axis=0))
    both = jnp.dot(table, jnp.concatenate([high, low, high], axis=0), preferred_element_type=F32)
    return both[:, :LANES], both[:, LANES:]


def tile_of(cols):
    for size in (2048, 1024, 512, 256, 128):
        if cols % size == 0:
            return size
    return cols


def kernel(
    plan,
    field_hbm, point_hbm, mixing_hbm, project_hbm, et_hbm, fine_hbm, coarse_hbm,
    image_out,
    value, local, et, fine, coarse, point, project, gains, gains_smem, raw, same, cross, kron, ahead, back, acc, hidden,
    total_image, packed, arrived, spread,
    field_sem, load_sem, sum_send, sum_recv, mix_send, mix_recv,
):
    groups, cores, owners, first_owner, per, sub, window, scale = plan
    channels, rows, cols = value.shape
    half_channels = channels // HALVES
    devices = groups * cores
    targets = owners * cores
    tile = tile_of(cols)
    clip = lax.axis_index("clip")
    row = lax.axis_index("trow")
    core = lax.axis_index("tcol")
    near = jnp.clip(row - first_owner, 0, owners - 1)
    is_owner = jnp.logical_and(row >= first_owner, row < first_owner + owners)
    me = row * cores + core
    block = core * owners + near
    start_mode = block * (per * KY)
    offset = lax.rem(start_mode, LANES)
    window_start = pl.multiple_of(start_mode - offset, LANES)

    loads = [
        pltpu.make_async_copy(fine_hbm, fine, load_sem.at[0]),
        pltpu.make_async_copy(coarse_hbm.at[row], coarse, load_sem.at[1]),
        pltpu.make_async_copy(et_hbm.at[core], et.at[pl.ds(0, 2 * KY)], load_sem.at[2]),
        pltpu.make_async_copy(point_hbm, point, load_sem.at[3]),
        pltpu.make_async_copy(project_hbm, project, load_sem.at[4]),
        pltpu.make_async_copy(mixing_hbm.at[:, :, :, :, pl.ds(window_start, window)], raw, load_sem.at[5]),
    ]
    for copy in loads[:3]:
        copy.start()

    def field_copy(c):
        return pltpu.make_async_copy(field_hbm.at[c], value.at[c], field_sem.at[c])

    for c in range(channels):
        field_copy(c).start()
    for copy in loads[3:]:
        copy.start()

    spread[...] = jnp.zeros_like(spread)
    et[2 * KY :, :] = jnp.zeros((LANES - 2 * KY, cols), BF16)

    def device_at(step):
        other = lax.rem(me + step, devices)
        return other // cores, lax.rem(other, cores)

    barrier = pltpu.get_barrier_semaphore()
    for step in range(1, devices):
        peer, peer_core = device_at(step)
        pl.semaphore_signal(barrier, inc=1, device_id=(clip, peer, peer_core), device_id_type=MESH)

    def used(ref):
        return ref.at[:, pl.ds(0, per), :]

    loads[0].wait()
    loads[1].wait()
    cc, cs = coarse[0:1, :], coarse[1:2, :]
    cosine = cc * fine[0] - cs * fine[1]
    sine = cs * fine[0] + cc * fine[1]
    high, low = split(jnp.concatenate([cosine, -sine], axis=1))
    back[...] = jnp.concatenate([high, high, low], axis=1)
    high, low = split(jnp.concatenate([cosine.T, sine.T], axis=1) * scale)
    ahead[...] = jnp.concatenate([high, high, low], axis=1)
    loads[2].wait()

    def columns_of(first, count):
        piece = value[first : first + count].reshape(count * rows, cols)
        result = lax.dot_general(piece, et[...], NT, preferred_element_type=F32)
        acc[first : first + count] = result.reshape(count, rows, LANES)

    def target_of(j):
        return lax.rem(near + owners // 2 + j // cores, owners), lax.rem(core + j, cores)

    def sum_copy(layer, half, j):
        q, k = target_of(j)
        slot = lax.rem(me - ((first_owner + q) * cores + k) + devices, devices) - 1
        slot = jnp.maximum(slot, 0)
        return pltpu.make_async_remote_copy(
            src_ref=used(packed.at[layer, half, k, q]),
            dst_ref=used(arrived.at[layer, half, slot]),
            send_sem=sum_send.at[layer, half, j],
            recv_sem=sum_recv.at[layer, half, slot],
            device_id=(clip, first_owner + q, k),
            device_id_type=MESH,
        )

    def for_targets(layer, half, act):
        for j in range(targets):
            q, k = target_of(j)

            @pl.when((first_owner + q) * cores + k != me)
            def _():
                act(sum_copy(layer, half, j))

    def transform_rows(layer, half):
        parts = []
        for p in range(0, half_channels, 2):
            c = half * half_channels + p
            parts.extend(two_transforms(ahead[...], acc[c], acc[c + 1]))
        for j, rows_j in enumerate(pack(parts)):
            packed[layer, half, :, :, j] = rows_j.reshape(cores, owners, sub, LANES)
        for_targets(layer, half, lambda copy: copy.start())

    def spread_copy(layer, half, step):
        peer, peer_core = device_at(step)
        return pltpu.make_async_remote_copy(
            src_ref=used(spread.at[layer, half, core, near]),
            dst_ref=used(spread.at[layer, half, core, near]),
            send_sem=mix_send.at[layer, half, step - 1],
            recv_sem=mix_recv.at[layer, half, core, near],
            device_id=(clip, peer, peer_core),
            device_id_type=MESH,
        )

    def arrival(ref, send_sem, recv_sem):
        peer, peer_core = device_at(1)
        return pltpu.make_async_remote_copy(
            src_ref=used(ref), dst_ref=used(ref), send_sem=send_sem, recv_sem=recv_sem,
            device_id=(clip, peer, peer_core), device_id_type=MESH,
        )

    order = sorted(range(1, devices), key=lambda step: abs(2 * step - devices))

    def mix(layer):
        @pl.when(is_owner)
        def _():
            plain = []
            for half in range(HALVES):
                sums = packed[layer, half, core, near]
                for slot in range(devices - 1):
                    arrival(
                        arrived.at[layer, half, slot], sum_send.at[layer, half, 0], sum_recv.at[layer, half, slot]
                    ).wait_recv()
                    sums = sums + arrived[layer, half, slot]
                plain.extend(unpack([sums[j] for j in range(TRIO)]))
            lane = lax.broadcasted_iota(jnp.int32, plain[0].shape, 1)
            swapped = [
                jnp.where(lane < KY, pltpu.roll(s, LANES - KY, 1), pltpu.roll(s, KY, 1)) for s in plain
            ]
            for half in range(HALVES):
                mixed = []
                for o in range(half * half_channels, (half + 1) * half_channels):
                    at = (layer * channels + o) * channels
                    result = same[at] * plain[0] + cross[at] * swapped[0]
                    for c in range(1, channels):
                        result = result + (same[at + c] * plain[c] + cross[at + c] * swapped[c])
                    mixed.append(result)
                for j, rows_j in enumerate(pack(mixed)):
                    spread[layer, half, core, near, j, 0:per, :] = rows_j[:per]
                for step in order:
                    spread_copy(layer, half, step).start()

    def prepare_hidden(layer, half):
        for k in range(cores):
            for q in range(owners):
                @pl.when((first_owner + q) * cores + k != me)
                def _():
                    arrival(
                        spread.at[layer, half, k, q], mix_send.at[layer, half, 0], mix_recv.at[layer, half, k, q]
                    ).wait_recv()
        parts = unpack([spread[layer, half, :, :, j].reshape(cores * owners * sub, LANES) for j in range(TRIO)])
        for p in range(0, half_channels, 2):
            for k, part in enumerate(two_transforms(back[...], parts[p], parts[p + 1])):
                hidden[half * half_channels + p + k] = part.astype(BF16)

    def kron_matrix(layer):
        size = channels * XB
        spot = lax.broadcasted_iota(jnp.int32, (size, channels), 0) // XB
        pick = (spot == lax.broadcasted_iota(jnp.int32, (size, channels), 1)).astype(F32).astype(BF16)
        wide = jnp.dot(pick, point[layer], preferred_element_type=F32).astype(BF16)
        full = lax.dot_general(wide, pick, NT, preferred_element_type=F32)
        at = lax.rem(lax.broadcasted_iota(jnp.int32, (size, size), 0), XB)
        to = lax.rem(lax.broadcasted_iota(jnp.int32, (size, size), 1), XB)
        kron[layer] = jnp.where(at == to, full, 0.0).astype(BF16)

    def mix_channels(layer):
        def step(i, carry):
            at = pl.multiple_of(i * tile, tile)
            for b in range(rows // XB):
                piece = value[:, b * XB : (b + 1) * XB, pl.ds(at, tile)].reshape(channels * XB, tile)
                result = jnp.dot(kron[layer], piece, preferred_element_type=F32)
                local[:, b * XB : (b + 1) * XB, pl.ds(at, tile)] = result.reshape(channels, XB, tile)
            return carry
        lax.fori_loop(0, cols // tile, step, 0)

    def updated(half, at, size):
        here = slice(half * half_channels, (half + 1) * half_channels)
        lhs = hidden[here].reshape(half_channels * rows, LANES)
        spectral = jnp.dot(lhs, et[:, at : at + size], preferred_element_type=F32)
        spectral = spectral.reshape(half_channels, rows, size)
        return jnp.tanh(local[here, :, at : at + size] + spectral * (1.0 / KY))

    def update(half):
        here = slice(half * half_channels, (half + 1) * half_channels)
        value[here] = updated(half, 0, cols).astype(BF16)

    def project_half(half):
        strip = min(cols, 512)
        factors = [gains_smem[0, half * half_channels + k] for k in range(half_channels)]
        for at in range(0, cols, strip):
            result = updated(half, at, strip)
            total = factors[0] * result[0]
            for k in range(1, half_channels):
                total = total + factors[k] * result[k]
            if half > 0:
                total = total_image[:, at : at + strip] + total
            if half + 1 < HALVES:
                total_image[:, at : at + strip] = total
            else:
                image_out[:, at : at + strip] = total.astype(BF16)

    def prepare_weights():
        loads[5].wait()
        count = LAYERS * 2 * channels
        flat = raw[...].astype(F32).reshape(count * channels, window).astype(BF16)
        mode = lax.broadcasted_iota(jnp.int32, (window, 2 * LANES), 0) - offset
        lane = lax.broadcasted_iota(jnp.int32, (window, 2 * LANES), 1)
        which = lane // LANES
        spot = lane - which * LANES
        wanted = which * KY + jnp.where(spot < KY, spot, spot - KY)
        wanted = jnp.where(spot < 2 * KY, wanted, -window * LANES)
        side = lax.broadcasted_iota(jnp.int32, (LAYERS * channels * channels, LANES), 1)
        for k in range(0, per, 2):
            choose = (mode - k * KY == wanted).astype(F32).astype(BF16)
            picked = jnp.dot(flat, choose, preferred_element_type=F32)
            picked = picked.reshape(LAYERS, 2, channels * channels, 2 * LANES)
            for n in range(2):
                lanes = slice(n * LANES, (n + 1) * LANES)
                real = picked[:, 0, :, lanes].reshape(LAYERS * channels * channels, LANES)
                imag = picked[:, 1, :, lanes].reshape(LAYERS * channels * channels, LANES)
                same[:, k + n, :] = real
                cross[:, k + n, :] = jnp.where(side < KY, -imag, imag)

    gain_copy = pltpu.make_async_copy(gains, gains_smem, load_sem.at[6])
    for half in range(HALVES):
        for c in range(half * half_channels, (half + 1) * half_channels, 2):
            field_copy(c).wait()
            field_copy(c + 1).wait()
            columns_of(c, 2)
        if half == 0:
            pl.semaphore_wait(barrier, devices - 1)
        transform_rows(0, half)
    loads[3].wait()
    loads[4].wait()
    gains[0:1, 0:channels] = project[...].astype(F32)
    gain_copy.start()
    for layer in range(LAYERS):
        kron_matrix(layer)
    prepare_weights()
    gain_copy.wait()

    for layer in range(LAYERS):
        last = layer + 1 == LAYERS
        if last:
            mix_channels(layer)
        mix(layer)
        if not last:
            mix_channels(layer)
        for half in range(HALVES):
            prepare_hidden(layer, half)
            if last:
                project_half(half)
            else:
                update(half)
                columns_of(half * half_channels, half_channels)
                transform_rows(layer + 1, half)

    for layer in range(LAYERS):
        for half in range(HALVES):
            for_targets(layer, half, lambda copy: copy.wait_send())

            @pl.when(is_owner)
            def _():
                for step in order:
                    spread_copy(layer, half, step).wait_send()


def body(groups, cores, field, pointwise, mixing, project):
    channels, rows, cols = field.shape
    owners = min(4, groups)
    first_owner = (groups - owners) // 2
    per = 2 * KY // (owners * cores)
    sub = -(-per // 8) * 8
    total_rows, total_cols = rows * groups, cols * cores
    scale = 1.0 / math.sqrt(total_rows * total_cols)
    modes = per * KY
    window = max(-(-(b * modes % LANES + modes) // LANES) * LANES for b in range(owners * cores))
    plan = (groups, cores, owners, first_owner, per, sub, window, scale)
    et = jnp.asarray(column_constant(total_cols, cores))
    fine, coarse = row_constants(total_rows, rows, groups, owners * cores, per, sub)
    fine, coarse = jnp.asarray(fine), jnp.asarray(coarse)

    hbm = pl.BlockSpec(memory_space=pltpu.HBM)
    dma = pltpu.SemaphoreType.DMA
    chunk = (TRIO, sub, LANES)
    pairs = LAYERS * channels * channels
    devices = groups * cores
    parts = LAYERS, HALVES
    return pl.pallas_call(
        functools.partial(kernel, plan),
        out_shape=jax.ShapeDtypeStruct((rows, cols), BF16),
        in_specs=[hbm] * 7,
        out_specs=pl.BlockSpec(memory_space=pltpu.VMEM),
        scratch_shapes=[
            pltpu.VMEM((channels, rows, cols), BF16),
            pltpu.VMEM((channels, rows, cols), F32),
            pltpu.VMEM((LANES, cols), BF16),
            pltpu.VMEM(fine.shape, F32),
            pltpu.VMEM(coarse.shape[1:], F32),
            pltpu.VMEM(pointwise.shape, BF16),
            pltpu.VMEM((1, channels), BF16),
            pltpu.VMEM((8, LANES), F32),
            pltpu.SMEM((8, LANES), F32),
            pltpu.VMEM(mixing.shape[:-1] + (window,), BF16),
            pltpu.VMEM((pairs, sub, LANES), F32),
            pltpu.VMEM((pairs, sub, LANES), F32),
            pltpu.VMEM((LAYERS, channels * XB, channels * XB), BF16),
            pltpu.VMEM((cores * owners * sub, 6 * rows), BF16),
            pltpu.VMEM((rows, 6 * cores * owners * sub), BF16),
            pltpu.VMEM((channels, rows, LANES), F32),
            pltpu.VMEM((channels, rows, LANES), BF16),
            pltpu.VMEM((rows, cols), F32),
            pltpu.VMEM(parts + (cores, owners) + chunk, F32),
            pltpu.VMEM(parts + (devices - 1,) + chunk, F32),
            pltpu.VMEM(parts + (cores, owners) + chunk, F32),
            dma((channels,)), dma((7,)),
            dma(parts + (owners * cores,)), dma(parts + (devices - 1,)),
            dma(parts + (devices - 1,)), dma(parts + (cores, owners)),
        ],
        compiler_params=pltpu.CompilerParams(
            collective_id=0, has_side_effects=True, vmem_limit_bytes=VMEM_BYTES
        ),
        name="operator",
    )(field, pointwise, mixing, project.reshape(1, channels), et, fine, coarse)


def solution(mesh):
    groups, cores = mesh.shape["trow"], mesh.shape["tcol"]
    in_specs = (P(None, ("clip", "trow"), "tcol"), P(), P(), P())
    out_specs = P(("clip", "trow"), "tcol")
    return jax.shard_map(
        functools.partial(body, groups, cores), mesh=mesh, in_specs=in_specs, out_specs=out_specs, check_vma=False
    )
```

time: 50.7 us -> 54.5 us (1.075)
  Pallas kernels: 48.2 us -> 52 us
    pallas_call x1, Pallas kernels: 48.2 us -> 52 us  [body(): pl.pallas_call(functools.partial(kernel, plan), out_shape=jax.ShapeDtypeS...]
where the time goes in v2:
time: 54.5 us; the launch traced here: 54.3 us
  Pallas kernels  52 us (95%)
  local copies, waits for them, and re-layouts  2.29 us (4%)
    pallas_call x1, Pallas kernels, body(): pl.pallas_call(functools.partial(kernel, plan), out_shape=jax.ShapeDtypeS...  52 us
    unnamed x1, local copies, waits for them, and re-layouts  2.29 us

profile of v2, /device:TPU:0, one launch (start us, length us, event | category | flops | bytes accessed | tf_op | source)
XLA Modules:
  0.0 54.3 jit_solution(12516440745747907304)
XLA Ops:
  0.0 52.0 %operator.1 = bf16[128,4096]{1,0:T(8,128)(2,1)} custom-call(bf16[8,128,4096]{2,1,0:T(8,128)(2,1)} %field_hbm.1, bf16[2,8,8]{2,1,0:T(8,128)(2,1)} %point_hbm.1, bf16[2,2,8,8,4608]{4,3,2,1,0:T(8,128)(2,1)} %mixing_hbm.1, bf16[1,8]{1,0:T(2,128)(2,1)} %bitcast.1, bf16[2,96,4096]{2,1,0:T(8,128)(2,1)} %constant.6.clone.et_hbm, ...), custom_call_target="tpu_custom_call" | custom-call | tf_op jit(solution)/shard_map/operator/pallas_call | solution.py:397
  52.0 2.3 %copy.9 = bf16[128,4096]{1,0:T(8,128)(2,1)} copy(bf16[128,4096]{1,0:T(8,128)(2,1)} %operator.1) | data formatting | bytes 2097152

commit v3 on v1

--- a/solution.py
+++ b/solution.py
@@ -95,7 +95,7 @@
     plan,
     field_hbm, point_hbm, mixing_hbm, project_hbm, et_hbm, fine_hbm, coarse_hbm,
     image_hbm,
-    value, local, et, fine, coarse, point, project, raw, same, cross, kron, ahead, back, acc, hidden, total_image, image,
+    value, local, et, fine, coarse, point, project, gains, gains_smem, raw, same, cross, kron, ahead, back, acc, hidden, total_image, image,
     packed, partner, mine, arrived, spread,
     field_sem, load_sem, pair_send, pair_recv, sum_send, sum_recv, mix_send, mix_recv, relay_send, relay_recv,
 ):
@@ -134,7 +134,6 @@
     for copy in loads[3:]:
         copy.start()
 
-    arrived[...] = jnp.zeros_like(arrived)
     spread[...] = jnp.zeros_like(spread)
     et[2 * KY :, :] = jnp.zeros((LANES - 2 * KY, cols), BF16)
 
@@ -319,35 +318,33 @@
             return carry
         lax.fori_loop(0, cols // local_tile, step, 0)
 
+    def half_slice(half):
+        return pl.ds(half * half_channels, half_channels)
+
     def updated(half, at):
-        mine_here = slice(half * half_channels, (half + 1) * half_channels)
-        lhs = hidden[mine_here].reshape(half_channels * rows, LANES)
+        lhs = hidden[half_slice(half)].reshape(half_channels * rows, LANES)
         spectral = jnp.dot(lhs, et[:, pl.ds(at, tile)], preferred_element_type=F32)
         spectral = spectral.reshape(half_channels, rows, tile)
-        return jnp.tanh(local[mine_here, :, pl.ds(at, tile)] + spectral * (1.0 / KY))
+        return jnp.tanh(local[half_slice(half), :, pl.ds(at, tile)] + spectral * (1.0 / KY))
 
     def update(half):
         def step(i, carry):
             at = pl.multiple_of(i * tile, tile)
-            value[half * half_channels : (half + 1) * half_channels, :, pl.ds(at, tile)] = updated(half, at).astype(BF16)
+            value[half_slice(half), :, pl.ds(at, tile)] = updated(half, at).astype(BF16)
             return carry
         lax.fori_loop(0, cols // tile, step, 0)
 
     def project_half(half):
-        gains = project[...].astype(F32)
+        factors = [gains_smem[0, half * half_channels + k] for k in range(half_channels)]
 
         def step(i, carry):
             at = pl.multiple_of(i * tile, tile)
             result = updated(half, at)
-            total = None if half == 0 else total_image[:, pl.ds(at, tile)]
+            total = total_image[:, pl.ds(at, tile)]
             for k in range(half_channels):
-                c = half * half_channels + k
-                term = gains[0:1, c : c + 1] * result[k]
-                total = term if total is None else total + term
-            if half + 1 < HALVES:
-                total_image[:, pl.ds(at, tile)] = total
-            else:
-                image[:, pl.ds(at, tile)] = total.astype(BF16)
+                total = total + factors[k] * result[k]
+            total_image[:, pl.ds(at, tile)] = total
+            image[:, pl.ds(at, tile)] = total.astype(BF16)
             return carry
         lax.fori_loop(0, cols // tile, step, 0)
 
@@ -373,6 +370,8 @@
                 same[:, k + n, :] = real
                 cross[:, k + n, :] = jnp.where(side < KY, -imag, imag)
 
+    gain_copy = pltpu.make_async_copy(gains, gains_smem, load_sem.at[6])
+
     def load_and_transform(c, carry):
         field_copy(c).wait()
         columns_of(c)
@@ -382,61 +381,94 @@
         columns_of(c)
         return carry
 
-    lax.fori_loop(0, half_channels, load_and_transform, 0)
-    pl.semaphore_wait(barrier, groups)
-    transform_rows(0, 0)
-    lax.fori_loop(half_channels, channels, load_and_transform, 0)
-    scatter_sums(0, 0)
-    transform_rows(0, 1)
+    def first_half(half, carry):
+        first = half * half_channels
+        lax.fori_loop(first, first + half_channels, load_and_transform, 0)
+
+        @pl.when(half == 0)
+        def _():
+            pl.semaphore_wait(barrier, groups)
+
+        @pl.when(half > 0)
+        def _():
+            scatter_sums(0, 0)
+        transform_rows(0, half)
+        return carry
+
+    lax.fori_loop(0, HALVES, first_half, 0)
     loads[3].wait()
     loads[4].wait()
-    for layer in range(LAYERS):
+    gains[0:1, 0:channels] = project[...].astype(F32)
+    gain_copy.start()
+    total_image[...] = jnp.zeros_like(total_image)
+
+    def prepare_kron(layer, carry):
         kron_matrix(layer)
+        return carry
+
+    lax.fori_loop(0, LAYERS, prepare_kron, 0)
     scatter_sums(0, 1)
     prepare_weights()
-
-    for layer in range(LAYERS):
-        last = layer + 1 == LAYERS
-        if last:
-            mix_channels(layer)
+    gain_copy.wait()
+
+    def one_layer(layer, carry):
         mix(layer)
-        if not last:
-            mix_channels(layer)
+        mix_channels(layer)
         relay(layer, 0)
-        prepare_hidden(layer, 0)
-        if last:
-            project_half(0)
-            relay(layer, 1)
-            prepare_hidden(layer, 1)
-            project_half(1)
-        else:
-            update(0)
-            relay(layer, 1)
-            lax.fori_loop(0, half_channels, transform_only, 0)
-            transform_rows(layer + 1, 0)
-            prepare_hidden(layer, 1)
-            update(1)
-            scatter_sums(layer + 1, 0)
-            lax.fori_loop(half_channels, channels, transform_only, 0)
-            transform_rows(layer + 1, 1)
+
+        def one_half(half, inner):
+            prepare_hidden(layer, half)
+
+            @pl.when(layer + 1 == LAYERS)
+            def _():
+                project_half(half)
+
+            @pl.when(layer + 1 < LAYERS)
+            def _():
+                update(half)
+
+            @pl.when(half == 0)
+            def _():
+                relay(layer, 1)
+
+            @pl.when(layer + 1 < LAYERS)
+            def _():
+                @pl.when(half > 0)
+                def _():
+                    scatter_sums(layer + 1, 0)
+                first = half * half_channels
+                lax.fori_loop(first, first + half_channels, transform_only, 0)
+                transform_rows(layer + 1, half)
+            return inner
+
+        lax.fori_loop(0, HALVES, one_half, 0)
+
+        @pl.when(layer + 1 < LAYERS)
+        def _():
             scatter_sums(layer + 1, 1)
+        return carry
+
+    lax.fori_loop(0, LAYERS, one_layer, 0)
 
     out = pltpu.make_async_copy(image, image_hbm, load_sem.at[6])
     out.start()
-    for layer in range(LAYERS):
-        for half in range(HALVES):
-            pair_copy(layer, half).wait_send()
-            for j in range(owners):
-                @pl.when(first_owner + sum_target(j) != row)
-                def _():
-                    sum_copy(layer, half, j).wait_send()
-            for q in range(owners):
-                relay_copy(layer, half, q).wait_send()
-
-            @pl.when(is_owner)
-            def _():
-                for j in order:
-                    spread_copy(layer, half, j).wait_send()
+    def drain(n, carry):
+        layer, half = n // HALVES, lax.rem(n, HALVES)
+        pair_copy(layer, half).wait_send()
+        for j in range(owners):
+            @pl.when(first_owner + sum_target(j) != row)
+            def _():
+                sum_copy(layer, half, j).wait_send()
+        for q in range(owners):
+            relay_copy(layer, half, q).wait_send()
+
+        @pl.when(is_owner)
+        def _():
+            for j in order:
+                spread_copy(layer, half, j).wait_send()
+        return carry
+
+    lax.fori_loop(0, LAYERS * HALVES, drain, 0)
     out.wait()
 
 
@@ -473,6 +505,8 @@
             pltpu.VMEM(coarse.shape[1:], F32),
             pltpu.VMEM(pointwise.shape, BF16),
             pltpu.VMEM((1, channels), BF16),
+            pltpu.VMEM((8, LANES), F32),
+            pltpu.SMEM((8, LANES), F32),
             pltpu.VMEM(mixing.shape[:-1] + (window,), BF16),
             pltpu.VMEM((pairs, sub, LANES), F32),
             pltpu.VMEM((pairs, sub, LANES), F32),

time: 50.7 us -> 50.7 us (level)
  no operation moved by 1% of the time
where the time goes in v3:
time: 50.7 us; the launch traced here: 50.6 us
  Pallas kernels  48.3 us (95%)
  local copies, waits for them, and re-layouts  2.29 us (5%)
    pallas_call x1, Pallas kernels, body(): pl.pallas_call(functools.partial(kernel, plan), out_shape=jax.ShapeDtypeS...  48.3 us
    unnamed x1, local copies, waits for them, and re-layouts  2.29 us

profile of v3, /device:TPU:0, one launch (start us, length us, event | category | flops | bytes accessed | tf_op | source)
XLA Modules:
  0.0 50.6 jit_solution(10757880864832488992)
XLA Ops:
  0.0 48.3 %operator.1 = bf16[128,4096]{1,0:T(8,128)(2,1)} custom-call(bf16[8,128,4096]{2,1,0:T(8,128)(2,1)} %field_hbm.1, bf16[2,8,8]{2,1,0:T(8,128)(2,1)} %point_hbm.1, bf16[2,2,8,8,4608]{4,3,2,1,0:T(8,128)(2,1)} %mixing_hbm.1, bf16[1,8]{1,0:T(2,128)(2,1)} %bitcast.1, bf16[2,96,4096]{2,1,0:T(8,128)(2,1)} %constant.6.clone.et_hbm, ...), custom_call_target="tpu_custom_call" | custom-call | tf_op jit(solution)/shard_map/operator/pallas_call | solution.py:495
  48.3 2.3 %copy.9 = bf16[128,4096]{1,0:T(8,128)(2,1)} copy(bf16[128,4096]{1,0:T(8,128)(2,1)} %operator.1) | data formatting | bytes 2097152
